TPU v7x, 256 devices: a whole 4x4x8 slice. The times are simulated.
256 devices in a mesh: pipe: 2 (over core), ctx: 32 (over y, z), tp: 4 (over x).
Axes of the slice: x: 4, y: 4, z: 8, core: 2. Of those that a mesh axis runs over, the one named last changes fastest.
Arguments:
- mamba_input: bfloat16 [2, 2048, 8192], P(None, 'ctx', 'tp')
- gate_input: bfloat16 [2, 2048, 8192], P(None, 'ctx', 'tp'), may hold values from -6 to 6
- bc_input: bfloat16 [2, 2048, 2, 2048], P(None, 'ctx', None, 'tp'), may hold values from -0.8984375 to 0.8984375
- step_raw: float32 [2, 2048, 64], P(None, 'ctx', 'tp'), may hold values from -4 to 4
- decay_log: float32 [64], P('tp')
- skip_gain: float32 [64], P('tp'), may hold values from 0.5 to 1.5
- conv_input: float32 [4, 8192], P(None, 'tp'), may hold values from -3 to 3
- conv_bc: float32 [4, 2, 2048], P(None, None, 'tp'), may hold values from -3 to 3
- norm_gain: float32 [8192], P('tp'), may hold values from 0.5 to 1.5
- keys_values: bfloat16 [2, 2048, 2, 1024], P(None, 'ctx', None, 'tp')
Outputs:
- attended: bfloat16 [2, 2048, 8192], P('pipe', 'ctx', 'tp')
All inputs are finite; a program needn't handle non-finite values.
Results may differ from a plain program's by a relative error of at most 0.006.
Values may be sent and summed in bfloat16 or wider, within the bound.
A program may use at most 320 MiB of HBM per device.

v0:
```python
import math

import jax
import jax.numpy as jnp
from jax import lax
from jax.sharding import PartitionSpec as P

STATE = 256


def passed_along(value, axis, steps):
    count = lax.axis_size(axis)
    first, last = (max(0, -steps), min(count, count - steps))
    return lax.ppermute(value, axis, [(source, source + steps) for source in range(first, last)])


def prefix(part, axis, combine, identity):
    place = lax.axis_index(axis)
    gathered = jax.tree.map(lambda a: lax.all_gather(a, axis), part)
    state = jax.tree.map(lambda a, e: jnp.zeros_like(a) + jnp.asarray(e, a.dtype), part, identity)

    def one(step, state):
        return combine(
            state, jax.tree.map(lambda a: lax.dynamic_index_in_dim(a, step, 0, False), gathered)
        )

    return lax.fori_loop(0, place, one, state)


def shifted(value, axis, steps):
    count = lax.axis_size(axis)
    pairs = [(source, (source + steps) % count) for source in range(count)]
    return lax.ppermute(value, axis, pairs)


def local(
    mamba_input,
    gate_input,
    bc_input,
    step_raw,
    decay_log,
    skip_gain,
    conv_input,
    conv_bc,
    norm_gain,
    keys_values,
):
    segment_index = lax.axis_index("pipe")
    row_count = mamba_input.shape[1]
    feature_width = mamba_input.shape[2]
    heads_here = step_raw.shape[2]
    groups_here = bc_input.shape[3] // STATE
    head_dim = feature_width // heads_here
    kv_here = keys_values.shape[3] // head_dim
    per_group = heads_here // groups_here
    per_kv = heads_here // kv_here
    taps = conv_input.shape[0]
    rim_rows = taps - 1
    position = lax.axis_index("ctx") * row_count
    factor = 1.0 / math.sqrt(head_dim)

    def causal_conv(current, previous, weight):
        joined = jnp.concatenate([previous, current], axis=0).astype(jnp.float32)
        running = weight[0] * joined[0:row_count]
        for offset in range(1, taps):
            running = running + weight[offset] * joined[offset : offset + row_count]
        return jax.nn.silu(running).astype(jnp.bfloat16)

    def combine(earlier, later):
        return (earlier[0] * later[0], later[0][..., None, None] * earlier[1] + later[1])

    def pick(array, micro_index):
        return lax.dynamic_slice_in_dim(array, micro_index, 1, 0)[0]

    def mamba_layer(micro_index):
        inputs = pick(mamba_input, micro_index)
        gates = pick(gate_input, micro_index)
        inbc = pick(bc_input, micro_index)
        raw_steps = pick(step_raw, micro_index)
        tail_input, tail_bc = passed_along(
            (inputs[row_count - rim_rows :], inbc[row_count - rim_rows :]), "ctx", 1
        )
        conv_out = causal_conv(inputs, tail_input, conv_input)
        bc_out = causal_conv(inbc, tail_bc, conv_bc)
        b_part = bc_out[:, 0].reshape(row_count, groups_here, STATE)
        c_part = bc_out[:, 1].reshape(row_count, groups_here, STATE)
        steps_dt = jax.nn.softplus(raw_steps).reshape(row_count, groups_here, per_group)
        decay_rate = -jnp.exp(decay_log).reshape(groups_here, per_group)
        cumul = jnp.cumsum(steps_dt * decay_rate, axis=0)
        order = jnp.arange(row_count, dtype=jnp.int32)
        lower_mask = (order[:, None] >= order[None, :])[:, :, None, None]
        decay_mat = jnp.exp(jnp.where(lower_mask, cumul[:, None] - cumul[None, :], -1e30))
        scores_cb = jnp.einsum("tgn,sgn->gts", c_part, b_part, preferred_element_type=jnp.float32)
        weights = (
            scores_cb[:, None]
            * jnp.transpose(decay_mat, (2, 3, 0, 1))
            * jnp.transpose(steps_dt, (1, 2, 0))[:, :, None, :]
        )
        weights = weights.astype(jnp.bfloat16)
        signal = conv_out.reshape(row_count, groups_here, per_group, head_dim)
        inner_part = jnp.einsum(
            "gkts,sgkp->tgkp", weights, signal, preferred_element_type=jnp.float32
        )
        tail_decay = jnp.exp(cumul[-1][None] - cumul) * steps_dt
        weighted = (signal.astype(jnp.float32) * tail_decay[..., None]).astype(jnp.bfloat16)
        local_state = jnp.einsum(
            "sgkp,sgn->gkpn", weighted, b_part, preferred_element_type=jnp.float32
        )
        block_decay = jnp.exp(cumul[-1])
        identity = (jnp.ones_like(block_decay), jnp.zeros_like(local_state))
        _, incoming = prefix((block_decay, local_state), "ctx", combine, identity)
        carried = jnp.exp(cumul)[..., None] * jnp.einsum(
            "tgn,gkpn->tgkp", c_part.astype(jnp.float32), incoming, precision=lax.Precision.HIGHEST
        )
        skip_view = skip_gain.reshape(groups_here, per_group)[None, :, :, None]
        mixed_out = inner_part + carried + skip_view * signal.astype(jnp.float32)
        gated = mixed_out.reshape(row_count, feature_width) * jax.nn.silu(gates.astype(jnp.float32))
        square_sum = lax.psum(jnp.sum(gated * gated, axis=1), "tp")
        norm_scale = lax.rsqrt(square_sum / (feature_width * lax.axis_size("tp")) + 1e-05)
        return (gated * norm_scale[:, None] * norm_gain).astype(jnp.bfloat16)

    def attend(queries, micro_kv):
        batch_count = queries.shape[0]
        query_view = queries.reshape(batch_count, row_count, kv_here, per_kv, head_dim)
        query_pos = position + jnp.arange(row_count, dtype=jnp.int32)
        start_max = jnp.full((batch_count, kv_here, per_kv, row_count), -1e30, jnp.float32)
        start_total = jnp.zeros((batch_count, kv_here, per_kv, row_count), jnp.float32)
        start_accum = jnp.zeros((batch_count, kv_here, per_kv, row_count, head_dim), jnp.float32)
        carry = (start_max, start_total, start_accum)
        piece = lax.all_gather(micro_kv, "ctx", axis=1, tiled=True)
        length = piece.shape[1]
        block_rows = math.gcd(length, 512)
        block_count = length // block_rows
        stacked = jnp.moveaxis(
            piece.reshape(batch_count, block_count, block_rows, 2, kv_here, head_dim), 1, 0
        )

        def one_block(held, item):
            block_index, key_block = item
            first_key = block_index * block_rows
            old_max, old_total, old_accum = held
            keys = key_block[:, :, 0]
            values = key_block[:, :, 1]
            logits = (
                jnp.einsum(
                    "btgkp,bsgp->bgkts", query_view, keys, preferred_element_type=jnp.float32
                )
                * factor
            )
            key_pos = first_key + jnp.arange(block_rows, dtype=jnp.int32)
            valid = key_pos[None, :] <= query_pos[:, None]
            masked = jnp.where(valid, logits, -1e30)
            new_max = jnp.maximum(old_max, jnp.max(masked, axis=-1))
            probs = jnp.where(valid, jnp.exp(logits - new_max[..., None]), 0.0)
            rescale = jnp.exp(old_max - new_max)
            new_total = old_total * rescale + jnp.sum(probs, axis=-1)
            product = jnp.einsum(
                "bgkts,bsgp->bgktp",
                probs.astype(jnp.bfloat16),
                values,
                preferred_element_type=jnp.float32,
            )
            new_accum = old_accum * rescale[..., None] + product
            held = (new_max, new_total, new_accum)
            return (held, None)

        carry, _ = lax.scan(one_block, carry, (jnp.arange(block_count, dtype=jnp.int32), stacked))
        final_max, final_total, final_accum = carry
        result = final_accum / final_total[..., None]
        return (
            jnp.transpose(result, (0, 3, 1, 2, 4))
            .reshape(batch_count, row_count, feature_width)
            .astype(jnp.bfloat16)
        )

    def pass_on(payload):
        return shifted(payload, "pipe", 1)

    is_first = segment_index == 0
    first_out = mamba_layer(0)
    arrived = pass_on(first_out)
    second_mamba = mamba_layer(1)
    first_attended = attend(arrived[None], keys_values[0:1])[0]
    second_out = jnp.where(is_first, second_mamba, first_attended)
    returned = pass_on(second_out)
    second_attended = attend(returned[None], keys_values[1:2])[0]
    result = jnp.where(is_first, returned, second_attended)
    return result[None]


def solution(mesh):
    in_specs = (
        P(None, "ctx", "tp"),
        P(None, "ctx", "tp"),
        P(None, "ctx", None, "tp"),
        P(None, "ctx", "tp"),
        P("tp"),
        P("tp"),
        P(None, "tp"),
        P(None, None, "tp"),
        P("tp"),
        P(None, "ctx", None, "tp"),
    )
    out_specs = P("pipe", "ctx", "tp")
    return jax.shard_map(local, mesh=mesh, in_specs=in_specs, out_specs=out_specs, check_vma=False)
```

profile of v0, /device:TPU:2, one launch (start us, length us, event | category | flops | bytes accessed | tf_op | source)
XLA Modules:
  0.0 1107.4 jit_solution(4514608604852893789)
XLA Ops:
  6.5 0.7 slice_bitcast_fusion.17
  7.3 3.8 collective-permute-start.1
  11.1 3.8 collective-permute-start.3
  14.9 0.8 slice_bitcast_fusion.15
  15.7 3.8 collective-permute-start
  19.6 5.0 collective-permute-start.2
  24.6 1.2 slice_bitcast_fusion.11
  26.5 0.8 broadcast_multiply_fusion.1
  27.8 1.1 slice_bitcast_fusion.9
  29.4 0.9 fusion.94
  30.3 1.1 slice_reduce_fusion.1
  32.3 2.1 fusion.70
  34.6 2.1 fusion.72
  37.7 46.7 %all_gather.26 = f32[32,2,8]{2,1,0:T(2,128)} all-gather(f32[1,2,8]{2,1,0:T(2,128)S(1)} %get-tuple-element.388), channel_id=1, replica_groups=mesh['pipe'=2,'ctx'=32,'tp'=4] {'ctx'}, dimensions={0}, use_global_device_ids=true | all-gather | bytes 2112 | tf_op jit(solution)/shard_map/all_gather | solution.py:19
  85.3 0.9 copy.185
  86.2 42.8 %all_gather.30 = f32[32,2,8]{2,1,0:T(2,128)S(1)} all-gather(f32[1,2,8]{2,1,0:T(2,128)S(1)} %get-tuple-element.390), channel_id=1, replica_groups=mesh['pipe'=2,'ctx'=32,'tp'=4] {'ctx'}, dimensions={0}, use_global_device_ids=true | all-gather | bytes 2112 | tf_op jit(solution)/shard_map/all_gather | solution.py:19
  129.2 0.9 copy.188
  130.4 333.5 %all-gather.13.cloned.1.call-done = f32[64,8,128,256]{3,2,1,0:T(8,128)} async-done(((f32[2,8,128,256]{3,2,1,0:T(8,128)}), f32[64,8,128,256]{3,2,1,0:T(8,128)}) %all-gather.13.cloned.1.call-update) | async-done | bytes 67108880 | tf_op jit(solution)/shard_map/all_gather | solution.py:19
  464.2 1.2 fusion.38
  465.5 1.2 multiply_reduce_fusion
  466.9 427.8 %all-gather.11.cloned.1.call-done = f32[64,8,128,256]{3,2,1,0:T(8,128)} async-done(((f32[2,8,128,256]{3,2,1,0:T(8,128)}), f32[64,8,128,256]{3,2,1,0:T(8,128)}) %all-gather.11.cloned.1.call-update) | async-done | bytes 67108880 | tf_op jit(solution)/shard_map/all_gather | solution.py:19
  895.0 1.2 fusion.39
  896.9 8.8 all-reduce
  906.1 66.4 %all-gather.7.cloned.1.call-done = bf16[1,2048,2,256]{3,2,0,1:T(2,128)(2,1)} async-done(((bf16[1,64,2,256]{3,2,0,1:T(2,128)(2,1)}), bf16[1,2048,2,256]{3,2,0,1:T(2,128)(2,1)}) %all-gather.7.cloned.1.call-update) | async-done | bytes 2097168 | tf_op jit(solution)/shard_map/all_gather | solution.py:130
  972.6 6.8 reshape.234
  979.3 1.1 copy.128
  980.6 25.5 %while.56 = (s32[]{:T(128)}, f32[1,2,8,64]{3,2,1,0:T(8,128)S(1)}, f32[1,2,8,64]{3,2,1,0:T(8,128)S(1)}, f32[1,2,8,64,128]{4,3,2,1,0:T(8,128)}, s32[4]{0:T(128)S(1...) while((s32[]{:T(128)}, f32[1,2,8,64]{3,2,1,0:T(8,128)S(1)}, ...), condition=%wide.region_13.14_spmd.clone, body=%wide.region_10.13_spmd.clone.sunk | while | flops 274635328 | bytes 10433181 | solution.py:167
  982.0 1.4 constant_dynamic-slice_fusion.4
  984.0 1.5 fusion.152
  987.6 1.4 constant_dynamic-slice_fusion.4
  989.6 2.5 fusion.152
  994.2 1.4 constant_dynamic-slice_fusion.4
  996.2 2.5 fusion.152
  1000.8 1.4 constant_dynamic-slice_fusion.4
  1002.9 2.5 fusion.152
  1006.1 1.3 fusion.92
  1008.2 58.2 %all-gather.9.cloned.1.call-done = bf16[1,2048,2,256]{3,2,0,1:T(2,128)(2,1)} async-done(((bf16[1,64,2,256]{3,2,0,1:T(2,128)(2,1)}), bf16[1,2048,2,256]{3,2,0,1:T(2,128)(2,1)}) %all-gather.9.cloned.1.call-update) | async-done | bytes 2097168 | tf_op jit(solution)/shard_map/all_gather | solution.py:130
  1066.4 6.8 reshape.235
  1073.3 25.3 %while.57 = (s32[]{:T(128)}, f32[1,2,8,64]{3,2,1,0:T(8,128)S(1)}, f32[1,2,8,64]{3,2,1,0:T(8,128)S(1)}, f32[1,2,8,64,128]{4,3,2,1,0:T(8,128)}, s32[4]{0:T(128)S(1...) while((s32[]{:T(128)}, f32[1,2,8,64]{3,2,1,0:T(8,128)S(1)}, ...), condition=%wide.region_17.18_spmd.clone, body=%wide.region_14.17_spmd.clone.sunk | while | flops 274635328 | bytes 10433181 | solution.py:167
  1074.6 1.4 constant_dynamic-slice_fusion.5
  1076.7 1.5 fusion.157
  1080.2 1.4 constant_dynamic-slice_fusion.5
  1082.2 2.5 fusion.157
  1086.8 1.4 constant_dynamic-slice_fusion.5
  1088.8 2.5 fusion.157
  1093.3 1.4 constant_dynamic-slice_fusion.5
  1095.4 2.5 fusion.157
  1098.6 1.2 fusion.93
  (191 shorter events, 24.5 us)
Async XLA Ops:
  6.5 22.4 %copy-start.5 = (f32[2,64,16]{1,2,0:T(8,128)S(1)}, f32[2,64,16]{1,2,0:T(8,128)}, u32[]{:S(2)}) copy-start(f32[2,64,16]{1,2,0:T(8,128)} %param.21) | copy-start | bytes 24580
  6.5 22.4 %copy-start.7 = (f32[4,2048]{1,0:T(4,128)S(1)}, f32[4,2048]{1,0:T(4,128)}, u32[]{:S(2)}) copy-start(f32[4,2048]{1,0:T(4,128)} %param.24) | copy-start | bytes 98308
  6.5 22.5 %copy-start.8 = (f32[4,2,512]{2,1,0:T(2,128)S(1)}, f32[4,2,512]{2,1,0:T(2,128)}, u32[]{:S(2)}) copy-start(f32[4,2,512]{2,1,0:T(2,128)} %param.25) | copy-start | bytes 49156
  6.5 457.4 %all-gather.13.cloned.1.call-start = ((), (), s32[]{:S(2)}) async-start(), calls=%async_computation.3 | async-start | bytes 69206016 | tf_op jit(solution)/shard_map/all_gather | solution.py:19
  7.3 21.8 %collective-permute-start.1 = (bf16[3,2,512]{2,1,0:T(2,128)(2,1)S(1)}, bf16[3,2,512]{2,1,0:T(2,128)(2,1)S(1)}, u32[]{:S(2)}, u32[]{:S(2)}) collective-permute-start(bf16[3,2,512]{2,1,0:T(2,128)(2,1)S(1)} %get-tuple-element.381), channel_id=1, source_target_pairs={{0,4},{4,8},{8,12},{12,16},{16,20},{20,24},{24,28},{28,32},{32,36}... | collective-permute-start | bytes 18440 | tf_op jit(solution)/shard_map/ppermute | solution.py:14
  11.1 18.2 %collective-permute-start.3 = (bf16[3,2,512]{2,1,0:T(2,128)(2,1)S(1)}, bf16[3,2,512]{2,1,0:T(2,128)(2,1)S(1)}, u32[]{:S(2)}, u32[]{:S(2)}) collective-permute-start(bf16[3,2,512]{2,1,0:T(2,128)(2,1)S(1)} %get-tuple-element.382), channel_id=1, source_target_pairs={{0,4},{4,8},{8,12},{12,16},{16,20},{20,24},{24,28},{28,32},{32,36}... | collective-permute-start | bytes 18440 | tf_op jit(solution)/shard_map/ppermute | solution.py:14
  15.7 15.7 %collective-permute-start = (bf16[3,2048]{1,0:T(4,128)(2,1)S(1)}, bf16[3,2048]{1,0:T(4,128)(2,1)S(1)}, u32[]{:S(2)}, u32[]{:S(2)}) collective-permute-start(bf16[3,2048]{1,0:T(4,128)(2,1)S(1)} %get-tuple-element.377), channel_id=1, source_target_pairs={{0,4},{4,8},{8,12},{12,16},{16,20},{20,24},{24,28},{28,32},{32,36}... | collective-permute-start | bytes 36872 | tf_op jit(solution)/shard_map/ppermute | solution.py:14
  19.6 11.9 %collective-permute-start.2 = (bf16[3,2048]{1,0:T(4,128)(2,1)S(1)}, bf16[3,2048]{1,0:T(4,128)(2,1)S(1)}, u32[]{:S(2)}, u32[]{:S(2)}) collective-permute-start(bf16[3,2048]{1,0:T(4,128)(2,1)S(1)} %get-tuple-element.378), channel_id=1, source_target_pairs={{0,4},{4,8},{8,12},{12,16},{16,20},{20,24},{24,28},{28,32},{32,36}... | collective-permute-start | bytes 36872 | tf_op jit(solution)/shard_map/ppermute | solution.py:14
  34.4 860.3 %all-gather.11.cloned.1.call-start = ((), (), s32[]{:S(2)}) async-start(), calls=%async_computation.2 | async-start | bytes 69206016 | tf_op jit(solution)/shard_map/all_gather | solution.py:19
  34.6 2.2 copy-start.4
  34.6 50.6 %copy-start = (bf16[2,64,2048]{2,1,0:T(8,128)(2,1)S(1)}, bf16[2,64,2048]{2,1,0:T(8,128)(2,1)}, u32[]{:S(2)}) copy-start(bf16[2,64,2048]{2,1,0:T(8,128)(2,1)} %param.19) | copy-start | bytes 1572868
  36.7 49.5 %copy-start.12 = (f32[16]{0:T(128)S(1)}, f32[16]{0:T(128)}, u32[]{:S(2)}) copy-start(f32[16]{0:T(128)} %param.23) | copy-start | bytes 196
  36.7 935.9 %all-gather.7.cloned.1.call-start = ((), (), s32[]{:S(2)}) async-start(), calls=%async_computation | async-start | bytes 2162688 | tf_op jit(solution)/shard_map/all_gather | solution.py:130
  37.5 1028.8 %all-gather.9.cloned.1.call-start = ((), (), s32[]{:S(2)}) async-start(), calls=%async_computation.1 | async-start | bytes 2162688 | tf_op jit(solution)/shard_map/all_gather | solution.py:130
  37.6 427.8 %copy-start.10 = (pred[64,64]{1,0:T(8,128)(4,1)}, pred[64,64]{1,0:T(8,128)(4,1)S(1)}, u32[]{:S(2)}) copy-start(pred[64,64]{1,0:T(8,128)(4,1)S(1)} %iota_compare_fusion) | copy-start | bytes 12292
  86.2 379.2 %copy-start.13 = (f32[2,8]{1,0:T(2,128)}, f32[2,8]{1,0:T(2,128)S(1)}, u32[]{:S(2)}) copy-start(f32[2,8]{1,0:T(2,128)S(1)} %mul.438) | copy-start | bytes 196
  464.2 1.2 copy-start.3
  895.0 1.3 copy-start.2
  895.0 1.3 copy-start.9
  895.0 1.3 copy-start.11
  895.0 1.3 copy-start.14
  896.3 0.6 copy-start.15
  896.3 9.4 copy-start.6
  906.0 74.5 %collective-permute-start.4 = (bf16[64,2048]{1,0:T(8,128)(2,1)S(1)}, bf16[64,2048]{1,0:T(8,128)(2,1)S(1)}, u32[]{:S(2)}, u32[]{:S(2)}) collective-permute-start(bf16[64,2048]{1,0:T(8,128)(2,1)S(1)} %fusion.68), channel_id=1, source_target_pairs={{0,128},{128,0},{1,129},{129,1},{2,130},{130,2},{3,131},{131,3},{4... | collective-permute-start | bytes 786440 | tf_op jit(solution)/shard_map/ppermute | solution.py:33
  1006.1 1.6 copy-start.1
  1008.1 65.1 %collective-permute-start.5 = (bf16[64,2048]{1,0:T(8,128)(2,1)S(1)}, bf16[64,2048]{1,0:T(8,128)(2,1)S(1)}, u32[]{:S(2)}, u32[]{:S(2)}) collective-permute-start(bf16[64,2048]{1,0:T(8,128)(2,1)S(1)} %fusion.96), channel_id=1, source_target_pairs={{0,128},{128,0},{1,129},{129,1},{2,130},{130,2},{3,131},{131,3},{4... | collective-permute-start | bytes 786440 | tf_op jit(solution)/shard_map/ppermute | solution.py:33
Sparse Core Ops, SparseCore 0:
  34.6 429.3 all-gather.12
  466.6 428.1 all-gather.10
  897.4 75.1 all-gather.6
  975.0 91.2 all-gather.8
where the time goes:
time: 1110 us
  waiting for transfers between devices  886 us (80%)
  blocking collectives  98.3 us (9%)
  local copies, waits for them, and re-layouts  42 us (4%)
  matrix products  30.7 us (3%)
  starting transfers between devices  16.8 us (2%)
  other arithmetic  13.8 us (1%)
  between operations  13.8 us (1%)
    all_gather x2, waiting for transfers between devices, prefix(): gathered = jax.tree.map(lambda a: lax.all_gather(a, axis), part)  761 us
    all_gather x2, waiting for transfers between devices, attend(): piece = lax.all_gather(micro_kv, 'ctx', axis=1, tiled=True)  125 us
    all_gather x2, blocking collectives, prefix(): gathered = jax.tree.map(lambda a: lax.all_gather(a, axis), part)  89.6 us
  transfers between devices with their start and end apart: 10, of which 4 were waited for; matrix products, arithmetic and copies ran while one was open for 5% of the time, Pallas kernels for 0%

commit v1 on v0

--- a/solution.py
+++ b/solution.py
@@ -14,25 +14,6 @@
     return lax.ppermute(value, axis, [(source, source + steps) for source in range(first, last)])
 
 
-def prefix(part, axis, combine, identity):
-    place = lax.axis_index(axis)
-    gathered = jax.tree.map(lambda a: lax.all_gather(a, axis), part)
-    state = jax.tree.map(lambda a, e: jnp.zeros_like(a) + jnp.asarray(e, a.dtype), part, identity)
-
-    def one(step, state):
-        return combine(
-            state, jax.tree.map(lambda a: lax.dynamic_index_in_dim(a, step, 0, False), gathered)
-        )
-
-    return lax.fori_loop(0, place, one, state)
-
-
-def shifted(value, axis, steps):
-    count = lax.axis_size(axis)
-    pairs = [(source, (source + steps) % count) for source in range(count)]
-    return lax.ppermute(value, axis, pairs)
-
-
 def local(
     mamba_input,
     gate_input,
@@ -45,7 +26,6 @@
     norm_gain,
     keys_values,
 ):
-    segment_index = lax.axis_index("pipe")
     row_count = mamba_input.shape[1]
     feature_width = mamba_input.shape[2]
     heads_here = step_raw.shape[2]
@@ -65,9 +45,6 @@
         for offset in range(1, taps):
             running = running + weight[offset] * joined[offset : offset + row_count]
         return jax.nn.silu(running).astype(jnp.bfloat16)
-
-    def combine(earlier, later):
-        return (earlier[0] * later[0], later[0][..., None, None] * earlier[1] + later[1])
 
     def pick(array, micro_index):
         return lax.dynamic_slice_in_dim(array, micro_index, 1, 0)[0]
@@ -107,8 +84,18 @@
             "sgkp,sgn->gkpn", weighted, b_part, preferred_element_type=jnp.float32
         )
         block_decay = jnp.exp(cumul[-1])
-        identity = (jnp.ones_like(block_decay), jnp.zeros_like(local_state))
-        _, incoming = prefix((block_decay, local_state), "ctx", combine, identity)
+        count = lax.axis_size("ctx")
+        slab = head_dim // count
+        pieces = local_state.reshape(heads_here, count, slab, STATE)
+        pieces = lax.all_to_all(pieces, "ctx", split_axis=1, concat_axis=0, tiled=False)
+        decays = lax.all_gather(block_decay.reshape(heads_here), "ctx")
+        held = jnp.zeros(pieces.shape[1:], jnp.float32)
+        before = []
+        for step in range(count):
+            before.append(held)
+            held = decays[step][:, None, None] * held + pieces[step]
+        incoming = lax.all_to_all(jnp.stack(before), "ctx", split_axis=0, concat_axis=1, tiled=False)
+        incoming = incoming.reshape(groups_here, per_group, head_dim, STATE)
         carried = jnp.exp(cumul)[..., None] * jnp.einsum(
             "tgn,gkpn->tgkp", c_part.astype(jnp.float32), incoming, precision=lax.Precision.HIGHEST
         )
@@ -173,19 +160,9 @@
             .astype(jnp.bfloat16)
         )
 
-    def pass_on(payload):
-        return shifted(payload, "pipe", 1)
-
-    is_first = segment_index == 0
-    first_out = mamba_layer(0)
-    arrived = pass_on(first_out)
-    second_mamba = mamba_layer(1)
-    first_attended = attend(arrived[None], keys_values[0:1])[0]
-    second_out = jnp.where(is_first, second_mamba, first_attended)
-    returned = pass_on(second_out)
-    second_attended = attend(returned[None], keys_values[1:2])[0]
-    result = jnp.where(is_first, returned, second_attended)
-    return result[None]
+    own = lax.axis_index("pipe")
+    queries = mamba_layer(own)
+    return attend(queries[None], lax.dynamic_slice_in_dim(keys_values, own, 1, 0))
 
 
 def solution(mesh):

time: 1110 us -> 260 us (0.23)
  waiting for transfers between devices: 886 us -> 36.1 us
  other arithmetic: 13.8 us -> 47.9 us
  matrix products: 30.7 us -> 13.8 us
  local copies, waits for them, and re-layouts: 42 us -> 30.8 us
    all_gather x2 -> x0, waiting for transfers between devices: 761 us -> none  [prefix(): gathered = jax.tree.map(lambda a: lax.all_gather(a, axis), part)]
    all_gather x2 -> x1, waiting for transfers between devices: 125 us -> 0.03 us  [attend(): piece = lax.all_gather(micro_kv, 'ctx', axis=1, tiled=True)]
    unnamed x8 -> x35, other arithmetic: 0.74 us -> 39.3 us
    all_to_all x0 -> x2, waiting for transfers between devices: none -> 36 us  [the longest x1 36 us: mamba_layer(): lax.all_to_all(jnp.stack(before), 'ctx', split_axis=0, concat_axis=1, til...]
    all_to_all x0 -> x2, starting transfers between devices: none -> 14.8 us  [the longest x1 9.82 us: mamba_layer(): lax.all_to_all(pieces, 'ctx', split_axis=1, concat_axis=0, tiled=False)]
    all_gather x2 -> x1, blocking collectives: 89.6 us -> 80.2 us  [mamba_layer(): decays = lax.all_gather(block_decay.reshape(heads_here), 'ctx')]
  transfers between devices with their start and end apart: 10 -> 5, of which waited for: 4 -> 1; matrix products, arithmetic and copies ran while one was open for 5% -> 21% of each run, Pallas kernels for 0% -> 0%
where the time goes in v1:
time: 260 us; the launch traced here: 257 us
  blocking collectives  89 us (34%)
  other arithmetic  47.9 us (18%)
  waiting for transfers between devices  36.1 us (14%)
  local copies, waits for them, and re-layouts  30.8 us (12%)
  starting transfers between devices  22.5 us (9%)
  matrix products  13.8 us (5%)
  between operations  13.7 us (5%)
  loops' own time  2.94 us (1%)
    all_gather x1, blocking collectives, mamba_layer(): decays = lax.all_gather(block_decay.reshape(heads_here), 'ctx')  80.2 us
    unnamed x35, other arithmetic  39.3 us
    all_to_all x1, waiting for transfers between devices, mamba_layer(): lax.all_to_all(jnp.stack(before), 'ctx', split_axis=0, concat_axis=1, til...  36 us
    all_to_all x1, starting transfers between devices, mamba_layer(): lax.all_to_all(pieces, 'ctx', split_axis=1, concat_axis=0, tiled=False)  9.82 us
    dot_general x4, matrix products, one_block(): jnp.einsum('bgkts,bsgp->bgktp', probs.astype(jnp.bfloat16), values, prefe...  8.99 us
    psum x1, blocking collectives, mamba_layer(): square_sum = lax.psum(jnp.sum(gated * gated, axis=1), 'tp')  8.81 us
    dynamic_slice x12, local copies, waits for them, and re-layouts, attend(): lax.scan(one_block, carry, (jnp.arange(block_count, dtype=jnp.int32), sta...  8.27 us
    ppermute x2, starting transfers between devices, passed_along(): lax.ppermute(value, axis, [(source, source + steps) for source in range(f...  7.65 us
  transfers between devices with their start and end apart: 5, of which 1 were waited for; matrix products, arithmetic and copies ran while one was open for 21% of the time, Pallas kernels for 0%

profile of v1, /device:TPU:2, one launch (start us, length us, event | category | flops | bytes accessed | tf_op | source)
XLA Modules:
  0.0 256.7 jit_solution(16350766651347257652)
XLA Ops:
  6.5 1.1 constant_dynamic-slice_fusion.1
  7.6 3.8 %collective-permute-start.1 = (bf16[3,2,512]{2,0,1:T(4,128)(2,1)S(1)}, bf16[3,2,512]{2,0,1:T(4,128)(2,1)S(1)}, u32[]{:S(2)}, u32[]{:S(2)}) collective-permute-start(bf16[3,2,512]{2,0,1:T(4,128)(2,1)S(1)} %slice_bitcast_fusion.35), channel_id=1, source_target_pairs={{0,4},{4,8},{8,12},{12,16},{16,20},{20,24},{24,28},{28,32},{32,36}... | collective-permute-start | bytes 18440 | tf_op jit(solution)/shard_map/ppermute | solution.py:14
  11.5 3.8 %collective-permute-start = (bf16[3,2048]{1,0:T(4,128)(2,1)S(1)}, bf16[3,2048]{1,0:T(4,128)(2,1)S(1)}, u32[]{:S(2)}, u32[]{:S(2)}) collective-permute-start(bf16[3,2048]{1,0:T(4,128)(2,1)S(1)} %dynamic-slice_bitcast_fusion.2), channel_id=1, source_target_pairs={{0,4},{4,8},{8,12},{12,16},{16,20},{20,24},{24,28},{28,32},{32,36}... | collective-permute-start | bytes 36872 | tf_op jit(solution)/shard_map/ppermute | solution.py:14
  17.2 0.9 fusion.103
  21.1 1.7 broadcast_in_dim_reshape.4
  22.8 3.5 %copy.222 = f32[1,16,32,4,256]{4,3,1,0,2:T(4,128)} copy(f32[1,16,32,4,256]{4,3,2,1,0:T(4,128)} %broadcast_in_dim_reshape.4) | data formatting | bytes 4194304 | tf_op jit(solution)/shard_map/broadcast_in_dim;reshape | solution.py:90
  26.3 9.8 %all-to-all-start = ((f32[1,16,32,4,256]{4,3,1,0,2:T(4,128)}), f32[1,16,32,4,256]{4,3,1,0,2:T(4,128)S(1)}, u32[]{:S(2)}, u32[]{:S(2)}) async-start(f32[1,16,32,4,256]{4,3,1,0,2:T(4,128)} %copy.222), calls=%async_computation | async-start | bytes 4194304 | tf_op jit(solution)/shard_map/all_to_all | solution.py:90
  37.0 80.2 %all-gather = f32[32,1,16]{2,1,0:T(1,128)S(1)} all-gather(f32[1,1,16]{2,1,0:T(1,128)S(1)} %reshape.2510), channel_id=1, replica_groups=mesh['pipe'=2,'ctx'=32,'tp'=4] {'ctx'}, dimensions={0}, use_global_device_ids=true | all-gather | bytes 2112 | tf_op jit(solution)/shard_map/all_gather | solution.py:91
  117.8 0.8 constant_dynamic-update-slice_fusion.30
  125.9 1.6 constant_dynamic-update-slice_fusion.19
  127.5 1.5 constant_dynamic-update-slice_fusion.18
  129.0 1.6 constant_dynamic-update-slice_fusion.17
  130.6 1.6 constant_dynamic-update-slice_fusion.16
  132.2 1.6 constant_dynamic-update-slice_fusion.15
  133.8 1.5 constant_dynamic-update-slice_fusion.14
  135.3 1.6 constant_dynamic-update-slice_fusion.13
  136.9 1.5 constant_dynamic-update-slice_fusion.12
  138.5 1.6 constant_dynamic-update-slice_fusion.11
  140.1 1.5 constant_dynamic-update-slice_fusion.10
  141.6 1.6 constant_dynamic-update-slice_fusion.9
  143.2 1.5 constant_dynamic-update-slice_fusion.8
  144.8 1.6 constant_dynamic-update-slice_fusion.7
  146.4 1.5 constant_dynamic-update-slice_fusion.6
  147.9 1.6 constant_dynamic-update-slice_fusion.5
  149.5 1.6 constant_dynamic-update-slice_fusion.4
  151.1 1.6 constant_dynamic-update-slice_fusion.3
  152.7 1.5 constant_dynamic-update-slice_fusion.2
  154.2 1.6 constant_dynamic-update-slice_fusion.1
  155.8 1.5 constant_dynamic-update-slice_fusion
  157.4 5.0 %all-to-all-start.1 = ((f32[32,16,1,4,256]{4,3,1,2,0:T(4,128)}), f32[32,16,1,4,256]{4,3,1,2,0:T(4,128)S(1)}, u32[]{:S(2)}, u32[]{:S(2)}) async-start(f32[32,16,1,4,256]{4,3,1,2,0:T(4,128)} %bitcast.542), calls=%async_computation.1 | async-start | bytes 4194304 | tf_op jit(solution)/shard_map/all_to_all | solution.py:97
  162.6 1.0 convert_bitcast_fusion
  163.6 0.9 copy.274
  164.8 6.8 %reshape.2585 = bf16[4,1,512,2,2,128]{5,4,3,2,0,1:T(2,128)(2,1)} reshape(bf16[1,2048,2,256]{3,2,0,1:T(2,128)(2,1)} %all-gather.3.cloned.1.call-done) | data formatting | bytes 4194304 | tf_op jit(solution)/shard_map/transpose;reshape | solution.py:121
  171.6 36.0 %all-to-all-done.1 = f32[32,16,1,4,256]{4,3,1,2,0:T(4,128)S(1)} async-done(((f32[32,16,1,4,256]{4,3,1,2,0:T(4,128)}), f32[32,16,1,4,256]{4,3,1,2,0:T(4,128)S(1)}, u32[]{:S(2)}, u32[]{:S(2)}) %all-to-all-start.1) | async-done | bytes 2097184 | tf_op jit(solution)/shard_map/all_to_all | solution.py:97
  207.6 1.9 copy.254
  209.5 2.0 reshape_squeeze.11
  211.4 1.2 fusion.19
  213.3 8.8 %psum.7 = f32[64]{0:T(128)S(1)} all-reduce(f32[64]{0:T(128)S(1)} %get-tuple-element.207), channel_id=1, replica_groups=mesh['pipe'=2,'ctx'=32,'tp'=4] {'tp'}, use_global_device_ids=true, to_apply=%region_2.3 | all-reduce | flops 64 | bytes 512 | tf_op jit(solution)/shard_map/psum | solution.py:105
  222.3 25.3 %while.15 = (s32[]{:T(128)}, f32[1,2,8,64]{3,2,1,0:T(8,128)S(1)}, f32[1,2,8,64]{3,2,1,0:T(8,128)S(1)}, f32[1,2,8,64,128]{4,3,2,1,0:T(8,128)}, s32[4]{0:T(128)S(1...) while((s32[]{:T(128)}, f32[1,2,8,64]{3,2,1,0:T(8,128)S(1)}, ...), condition=%wide.region_6.7_spmd.clone, body=%wide.region_3.6_spmd.clone.sunk | while | flops 274635328 | bytes 10433181 | solution.py:154
  223.6 1.4 constant_dynamic-slice_fusion.3
  225.7 1.5 fusion.116
  229.2 1.4 constant_dynamic-slice_fusion.3
  231.2 2.5 fusion.116
  235.8 1.4 constant_dynamic-slice_fusion.3
  237.8 2.5 fusion.116
  242.4 1.4 constant_dynamic-slice_fusion.3
  244.4 2.5 fusion.116
  247.6 1.2 fusion.39
  (110 shorter events, 23.5 us)
Async XLA Ops:
  6.5 4.9 %copy-start = (bf16[2,64,2048]{2,1,0:T(8,128)(2,1)S(1)}, bf16[2,64,2048]{2,1,0:T(8,128)(2,1)}, u32[]{:S(2)}) copy-start(bf16[2,64,2048]{2,1,0:T(8,128)(2,1)} %param.12) | copy-start | bytes 1572868
  7.6 12.0 %collective-permute-start.1 = (bf16[3,2,512]{2,0,1:T(4,128)(2,1)S(1)}, bf16[3,2,512]{2,0,1:T(4,128)(2,1)S(1)}, u32[]{:S(2)}, u32[]{:S(2)}) collective-permute-start(bf16[3,2,512]{2,0,1:T(4,128)(2,1)S(1)} %slice_bitcast_fusion.35), channel_id=1, source_target_pairs={{0,4},{4,8},{8,12},{12,16},{16,20},{20,24},{24,28},{28,32},{32,36}... | collective-permute-start | bytes 18440 | tf_op jit(solution)/shard_map/ppermute | solution.py:14
  11.5 8.4 %collective-permute-start = (bf16[3,2048]{1,0:T(4,128)(2,1)S(1)}, bf16[3,2048]{1,0:T(4,128)(2,1)S(1)}, u32[]{:S(2)}, u32[]{:S(2)}) collective-permute-start(bf16[3,2048]{1,0:T(4,128)(2,1)S(1)} %dynamic-slice_bitcast_fusion.2), channel_id=1, source_target_pairs={{0,4},{4,8},{8,12},{12,16},{16,20},{20,24},{24,28},{28,32},{32,36}... | collective-permute-start | bytes 36872 | tf_op jit(solution)/shard_map/ppermute | solution.py:14
  26.3 9.9 %copy-start.3 = (bf16[2,64,2,256]{3,2,1,0:T(2,128)(2,1)S(1)}, bf16[2,64,2,256]{3,2,1,0:T(2,128)(2,1)}, u32[]{:S(2)}) copy-start(bf16[2,64,2,256]{3,2,1,0:T(2,128)(2,1)} %param.21) | copy-start | bytes 393220
  26.3 91.5 %all-to-all-start = ((f32[1,16,32,4,256]{4,3,1,0,2:T(4,128)}), f32[1,16,32,4,256]{4,3,1,0,2:T(4,128)S(1)}, u32[]{:S(2)}, u32[]{:S(2)}) async-start(f32[1,16,32,4,256]{4,3,1,0,2:T(4,128)} %copy.222), calls=%async_computation | async-start | bytes 4194304 | tf_op jit(solution)/shard_map/all_to_all | solution.py:90
  36.1 128.7 %all-gather.3.cloned.1.call-start = ((), (), s32[]{:S(2)}) async-start(), calls=%async_computation.2 | async-start | bytes 2162688 | tf_op jit(solution)/shard_map/all_gather | solution.py:117
  117.8 8.0 %copy-start.1 = (f32[1,16,32,4,256]{4,3,1,0,2:T(4,128)}, f32[1,16,32,4,256]{4,3,1,0,2:T(4,128)S(1)}, u32[]{:S(2)}) copy-start(f32[1,16,32,4,256]{4,3,1,0,2:T(4,128)S(1)} %all-to-all-done) | copy-start | bytes 6291460
  157.4 50.2 %all-to-all-start.1 = ((f32[32,16,1,4,256]{4,3,1,2,0:T(4,128)}), f32[32,16,1,4,256]{4,3,1,2,0:T(4,128)S(1)}, u32[]{:S(2)}, u32[]{:S(2)}) async-start(f32[32,16,1,4,256]{4,3,1,2,0:T(4,128)} %bitcast.542), calls=%async_computation.1 | async-start | bytes 4194304 | tf_op jit(solution)/shard_map/all_to_all | solution.py:97
  162.4 2.1 copy-start.5
  211.4 1.2 copy-start.2
  212.7 9.4 %copy-start.4 = (f32[2048]{0:T(1024)S(1)}, f32[2048]{0:T(1024)}, u32[]{:S(2)}) copy-start(f32[2048]{0:T(1024)} %param.20) | copy-start | bytes 24580
Sparse Core Ops, SparseCore 0:
  39.5 82.2 all-gather.2
